TPU v7x, 32 devices: a whole 2x2x4 slice. The times are simulated.
32 devices in a mesh: grp: 2 (over x), ctg: 16 (over z, y, core).
Axes of the slice: x: 2, y: 2, z: 4, core: 2. Of those that a mesh axis runs over, the one named last changes fastest.
Arguments:
- flow_tiles: bfloat16 [128, 256, 3072], P('ctg'), may hold values from -0.109375 to 0.109375
- tile_pattern: int32 [128, 2, 24], P('ctg'), may hold values 0 or 1
- monitored: int32 [128, 256], P('ctg'), may hold values from 0 to 16383
- ratings: float32 [16384], replicated, may hold values from 0.3 to 3
- base_flow: float32 [64, 128, 256], P('grp', 'ctg'), parts along dimension 0, may hold values from -6 to 6
- unit_cost: float32 [64, 3072], P(('grp', 'ctg')), parts along dimension 0, may hold values from -6 to 6
- unit_floor: float32 [3072], replicated, may hold values from 0 to 0.5
- unit_span: float32 [3072], replicated, may hold values from 0.5 to 2
- ramp_limit: float32 [3072], replicated, may hold values from 0.05 to 0.5
- ramp_mask: int32 [3072], replicated, may hold values 0 or 1
- demand: float32 [64], P(('grp', 'ctg')), parts along dimension 0, may hold values from 1228.8 to 2457.6
- start_output: float32 [64, 3072], P(('grp', 'ctg')), parts along dimension 0, may hold values from 0 to 1.5
- start_flow_dual: float32 [64, 128, 256], P('grp', 'ctg'), parts along dimension 0, may hold values from -2 to 2
- start_ramp_dual: float32 [64, 3072], P(('grp', 'ctg')), parts along dimension 0, may hold values from -3 to 3
Outputs:
- output_levels: float32 [64, 3072], P(('grp', 'ctg')), parts along dimension 0
- flow_dual: float32 [64, 128, 256], P('grp', 'ctg'), parts along dimension 0
- ramp_dual: float32 [64, 3072], P(('grp', 'ctg')), parts along dimension 0
- balance_price: float32 [64], P(('grp', 'ctg')), parts along dimension 0
There are 2 independent parts, one for each index of `grp`. A program takes and returns all parts, laid end to end along the dimension named above; an argument that names none is the same for every part. Nothing has to cross between parts.
All inputs are finite; a program needn't handle non-finite values. No bound on the sum of `tile_pattern` on one device may be relied on, other than what follows from the above.
Results may differ from a plain program's by a relative error of at most 0.0045.
Values may be sent and summed in bfloat16 or wider, within the bound.
A program may use at most 128 MiB of HBM per device.

v0:
```python
import math

import jax
import jax.numpy as jnp
from jax import lax
from jax.sharding import PartitionSpec as P

ITERS = 4


def mask_tiles(flow_tiles, tile_pattern):
    ctg_count, line_count, unit_count = flow_tiles.shape
    blocks = flow_tiles.reshape(ctg_count, line_count // 128, 128, unit_count // 128, 128)
    gates = tile_pattern.astype(jnp.bfloat16)[:, :, None, :, None]
    return (blocks * gates).reshape(ctg_count, line_count, unit_count)


def dual_prox(trial, dual_step, lower_side, upper_side):
    return trial - dual_step * jnp.clip(trial / dual_step, lower_side, upper_side)


def body(
    flow_tiles,
    tile_pattern,
    monitored,
    ratings,
    base_flow,
    unit_cost,
    unit_floor,
    unit_span,
    ramp_limit,
    ramp_mask,
    demand,
    start_output,
    start_flow_dual,
    start_ramp_dual,
):
    ctg_count, line_count, unit_count = flow_tiles.shape
    devices = lax.axis_size("ctg")
    position = lax.axis_index("ctg")
    masked = mask_tiles(flow_tiles, tile_pattern)
    flow_limit = ratings[monitored]
    flow_lower = base_flow - flow_limit[None]
    flow_upper = base_flow + flow_limit[None]
    step_size = 0.5 / (2.0 + math.sqrt(ctg_count * devices * line_count / unit_count))
    balance = 1.0 / math.sqrt(unit_count)
    ceiling = unit_floor + unit_span
    ramp_on = ramp_mask.astype(jnp.float32)
    weight = jnp.float32(1.0)
    hour_rows = start_output.shape[0]
    zero_row = jnp.zeros((1, unit_count), jnp.float32)
    flow_dual = start_flow_dual
    levels, costs, ramp_dual, demands = (
        lax.all_gather(start_output, "ctg", axis=0, tiled=True),
        lax.all_gather(unit_cost, "ctg", axis=0, tiled=True),
        lax.all_gather(start_ramp_dual, "ctg", axis=0, tiled=True),
        lax.all_gather(demand, "ctg", axis=0, tiled=True),
    )
    balance_price = jnp.zeros(demands.shape, jnp.float32)
    for iteration in range(ITERS):
        primal_step = step_size / weight
        dual_step = step_size * weight
        dual_half = flow_dual.astype(jnp.bfloat16)
        own_term = jnp.einsum("tkm,kmu->tu", dual_half, masked, preferred_element_type=jnp.float32)
        pulled = lax.psum(own_term.astype(jnp.bfloat16), "ctg").astype(jnp.float32)
        before = jnp.concatenate([zero_row, ramp_dual[:-1]], axis=0)
        gradient = (
            costs + pulled + ramp_on * (before - ramp_dual) + balance * balance_price[:, None]
        )
        moved = jnp.clip(levels - primal_step * gradient, unit_floor, ceiling)
        extended = 2.0 * moved - levels
        extended_half = extended.astype(jnp.bfloat16)
        flows = jnp.einsum("kmu,tu->tkm", masked, extended_half, preferred_element_type=jnp.float32)
        dual_new = dual_prox(flow_dual + dual_step * flows, dual_step, flow_lower, flow_upper)
        change = ramp_on * jnp.concatenate([extended[1:] - extended[:-1], zero_row], axis=0)
        ramp_new = dual_prox(ramp_dual + dual_step * change, dual_step, -ramp_limit, ramp_limit)
        balance_row = balance * (jnp.sum(extended, axis=1) - demands)
        price_new = balance_price + dual_step * balance_row
        if iteration < ITERS - 1:
            primal_sq = jnp.sum((moved - levels) ** 2)
            flow_sq = lax.psum(jnp.sum((dual_new - flow_dual) ** 2), "ctg")
            dual_sq = (
                flow_sq
                + jnp.sum((ramp_new - ramp_dual) ** 2)
                + jnp.sum((price_new - balance_price) ** 2)
            )
            weight = jnp.sqrt(weight) * ((dual_sq + 1e-06) / (primal_sq + 1e-06)) ** 0.25
        levels = moved
        flow_dual = dual_new
        ramp_dual = ramp_new
        balance_price = price_new
    first_hour = position * hour_rows
    own_levels = lax.dynamic_slice_in_dim(levels, first_hour, hour_rows, 0)
    own_ramp = lax.dynamic_slice_in_dim(ramp_dual, first_hour, hour_rows, 0)
    own_price = lax.dynamic_slice_in_dim(balance_price, first_hour, hour_rows, 0)
    return (own_levels, flow_dual, own_ramp, own_price)


def solution(mesh):
    return jax.shard_map(
        body,
        mesh=mesh,
        in_specs=(
            P("ctg", None, None),
            P("ctg", None, None),
            P("ctg", None),
            P(),
            P("grp", "ctg", None),
            P(("grp", "ctg"), None),
            P(),
            P(),
            P(),
            P(),
            P(("grp", "ctg")),
            P(("grp", "ctg"), None),
            P("grp", "ctg", None),
            P(("grp", "ctg"), None),
        ),
        out_specs=(
            P(("grp", "ctg"), None),
            P("grp", "ctg", None),
            P(("grp", "ctg"), None),
            P(("grp", "ctg")),
        ),
        check_vma=False,
    )
```

profile of v0, /device:TPU:0, one launch (start us, length us, event | category | flops | bytes accessed | tf_op | source)
XLA Modules:
  0.0 492.0 jit_solution(2523741557012118708)
XLA Ops:
  7.9 6.3 %mul.232 = bf16[8,2,128,24,128]{4,3,2,1,0:T(8,128)(2,1)} broadcast(bf16[8,2,24]{2,1,0:T(2,128)(2,1)S(1)} %convert_element_type.57), dimensions={0,1,3} | broadcast | bytes 12583680 | tf_op jit(solution)/shard_map/mul | solution.py:15
  14.2 19.3 %mul.233 = bf16[8,256,3072]{2,1,0:T(8,128)(2,1)} reshape(bf16[8,2,128,24,128]{4,3,2,1,0:T(8,128)(2,1)} %mul.232) | data formatting | bytes 25165824 | tf_op jit(solution)/shard_map/mul | solution.py:15
  33.5 11.4 %mul.234 = bf16[8,256,3072]{2,1,0:T(8,128)(2,1)S(1)} multiply(bf16[8,256,3072]{2,1,0:T(8,128)(2,1)} %param.14, bf16[8,256,3072]{2,1,0:T(8,128)(2,1)} %mul.233) | non-fusion elementwise | flops 6291456 | bytes 37748736 | tf_op jit(solution)/shard_map/mul | solution.py:15
  45.0 4.6 copy-done.1
  49.7 2.9 fusion.4
  52.7 24.2 %all-gather.1 = f32[16,2,3072]{2,1,0:T(2,128)S(1)} all-gather(f32[1,2,3072]{2,1,0:T(2,128)S(1)} %bitcast.64), channel_id=1, replica_groups=mesh['grp'=2,'ctg'=16] {'ctg'}, dimensions={0}, use_global_device_ids=true | all-gather | bytes 417792 | tf_op jit(solution)/shard_map/all_gather | solution.py:55
  77.2 18.6 %all-gather.2 = f32[16,2,3072]{2,1,0:T(2,128)S(1)} all-gather(f32[1,2,3072]{2,1,0:T(2,128)S(1)} %bitcast.65), channel_id=1, replica_groups=mesh['grp'=2,'ctg'=16] {'ctg'}, dimensions={0}, use_global_device_ids=true | all-gather | bytes 417792 | tf_op jit(solution)/shard_map/all_gather | solution.py:56
  96.2 20.1 %all-gather = f32[16,2,3072]{2,1,0:T(2,128)S(1)} all-gather(f32[1,2,3072]{2,1,0:T(2,128)S(1)} %bitcast.66), channel_id=1, replica_groups=mesh['grp'=2,'ctg'=16] {'ctg'}, dimensions={0}, use_global_device_ids=true | all-gather | bytes 417792 | tf_op jit(solution)/shard_map/all_gather | solution.py:54
  116.6 11.8 %gather_fusion = f32[2048]{0:T(1024)S(1)} fusion(f32[16384]{0:T(1024)S(1)} %copy-done, s32[2048]{0:T(1024)S(1)} %broadcast_clamp_fusion), kind=kCustom, calls=%fused_computation | custom fusion | bytes 24576 | tf_op jit(solution)/shard_map/gather | solution.py:42
  129.9 16.5 %all-reduce.15.cloned.1.call-done = bf16[32,3072]{1,0:T(8,128)(2,1)} async-done(((bf16[32,3072]{1,0:T(8,128)(2,1)}), bf16[32,3072]{1,0:T(8,128)(2,1)}) %all-reduce.15.cloned.1.call-update) | async-done | bytes 196624 | tf_op jit(solution)/shard_map/psum | solution.py:65
  148.4 9.1 %multiply_reduce_fusion.8 = (f32[]{:T(128)}, f32[32,8,256]{2,0,1:T(8,128)S(1)}) fusion(f32[32,8,256]{2,1,0:T(8,128)S(1)} %copy-done.3, f32[8,256]{1,0:T(8,128)S(1)} %reshape.25, f32[32,8,256]{2,1,0:T(8,128)S(1)} %copy-done.2, bf16[8,256,3072]{2,1,0:T(8,128)(2,1)} %copy-done.1, f32[32,3072]{1,0:T(8,128)S(1)} %get-tuple-element.42), kind=kOutput, calls=%fused_computation.47 | convolution fusion | flops 403537920 | bytes 13770756 | tf_op jit(solution)/shard_map/kmu,tu->tkm/dot_general | solution.py:73
  157.5 7.5 %fusion = bf16[32,3072]{1,0:T(8,128)(2,1)} fusion(bf16[8,256,3072]{2,1,0:T(8,128)(2,1)} %copy-done.1, f32[32,8,256]{2,0,1:T(8,128)S(1)} %get-tuple-element.46, f32[32,8,256]{2,1,0:T(8,128)S(1)} %copy-done.2, f32[8,256]{1,0:T(8,128)S(1)} %reshape.25), kind=kOutput, calls=%fused_computation.5 | convolution fusion | flops 403275776 | bytes 13312000 | tf_op jit(solution)/shard_map/tkm,kmu->tu/dot_general | solution.py:64
  165.1 31.2 %all-reduce.9 = (f32[32]{0:T(128)S(1)}, f32[]{:T(128)}) all-reduce(f32[32]{0:T(128)S(1)} %dynamic-update-slice, f32[]{:T(128)} %get-tuple-element.45), channel_id=1, replica_groups=mesh['grp'=2,'ctg'=16] {'ctg'}, use_global_device_ids=true, to_apply=%add.8 | all-reduce | flops 33 | bytes 264
  200.3 54.7 %all-reduce.17.cloned.1.call-done = bf16[32,3072]{1,0:T(8,128)(2,1)} async-done(((bf16[32,3072]{1,0:T(8,128)(2,1)}), bf16[32,3072]{1,0:T(8,128)(2,1)}) %all-reduce.17.cloned.1.call-update) | async-done | bytes 196624 | tf_op jit(solution)/shard_map/psum | solution.py:65
  257.0 9.1 %multiply_reduce_fusion.7 = (f32[]{:T(128)}, f32[32,8,256]{2,0,1:T(8,128)S(1)}) fusion(f32[32,8,256]{2,0,1:T(8,128)S(1)} %get-tuple-element.46, f32[]{:T(128)S(6)} %mul.251, f32[8,256]{1,0:T(8,128)S(1)} %reshape.25, f32[32,8,256]{2,1,0:T(8,128)S(1)} %copy-done.2, bf16[8,256,3072]{2,1,0:T(8,128)(2,1)} %copy-done.1, f32[32,3072]{1,0:T(8,128)S(1)} %get-tuple-element.36), kind=kOutput, calls=%fused_computation.44 | convolution fusion | flops 403865600 | bytes 13770760 | tf_op jit(solution)/shard_map/kmu,tu->tkm/dot_general | solution.py:73
  266.8 7.5 %fusion.1 = bf16[32,3072]{1,0:T(8,128)(2,1)} fusion(bf16[8,256,3072]{2,1,0:T(8,128)(2,1)} %copy-done.1, f32[32,8,256]{2,0,1:T(8,128)S(1)} %get-tuple-element.48, f32[]{:T(128)S(6)} %mul.251, f32[32,8,256]{2,1,0:T(8,128)S(1)} %copy-done.2, f32[8,256]{1,0:T(8,128)S(1)} %reshape.25), kind=kOutput, calls=%fused_computation.6 | convolution fusion | flops 403275776 | bytes 13312004 | tf_op jit(solution)/shard_map/tkm,kmu->tu/dot_general | solution.py:64
  275.0 31.3 %psum.52 = f32[]{:T(128)} all-reduce(f32[]{:T(128)} %get-tuple-element.47), channel_id=1, replica_groups=mesh['grp'=2,'ctg'=16] {'ctg'}, use_global_device_ids=true, to_apply=%region_9.10 | all-reduce | flops 1 | bytes 8 | tf_op jit(solution)/shard_map/psum | solution.py:81
  309.1 55.2 %all-reduce.19.cloned.1.call-done = bf16[32,3072]{1,0:T(8,128)(2,1)} async-done(((bf16[32,3072]{1,0:T(8,128)(2,1)}), bf16[32,3072]{1,0:T(8,128)(2,1)}) %all-reduce.19.cloned.1.call-update) | async-done | bytes 196624 | tf_op jit(solution)/shard_map/psum | solution.py:65
  364.3 1.7 multiply_reduce_fusion
  366.3 9.1 %multiply_reduce_fusion.6 = (f32[]{:T(128)}, f32[32,8,256]{2,0,1:T(8,128)S(1)}) fusion(f32[32,8,256]{2,0,1:T(8,128)S(1)} %get-tuple-element.48, f32[]{:T(128)S(6)} %mul.268, f32[]{:T(128)S(6)} %mul.251, f32[8,256]{1,0:T(8,128)S(1)} %reshape.25, f32[32,8,256]{2,1,0:T(8,128)S(1)} %copy-done.2, bf16[8,256,3072]{2,1,0:T(8,128)(2,1)} %copy-done.1, ...), kind=kOutput, calls=%fused_computation.41 | convolution fusion | flops 403865600 | bytes 13770764 | tf_op jit(solution)/shard_map/kmu,tu->tkm/dot_general | solution.py:73
  376.1 7.5 %fusion.2 = bf16[32,3072]{1,0:T(8,128)(2,1)} fusion(bf16[8,256,3072]{2,1,0:T(8,128)(2,1)} %copy-done.1, f32[32,8,256]{2,0,1:T(8,128)S(1)} %get-tuple-element.50, f32[]{:T(128)S(6)} %mul.268, f32[32,8,256]{2,1,0:T(8,128)S(1)} %copy-done.2, f32[8,256]{1,0:T(8,128)S(1)} %reshape.25), kind=kOutput, calls=%fused_computation.7 | convolution fusion | flops 403275776 | bytes 13312004 | tf_op jit(solution)/shard_map/tkm,kmu->tu/dot_general | solution.py:64
  384.2 31.1 %psum.54 = f32[]{:T(128)} all-reduce(f32[]{:T(128)} %get-tuple-element.49), channel_id=1, replica_groups=mesh['grp'=2,'ctg'=16] {'ctg'}, use_global_device_ids=true, to_apply=%region_16.17 | all-reduce | flops 1 | bytes 8 | tf_op jit(solution)/shard_map/psum | solution.py:81
  418.0 55.5 %all-reduce.21.cloned.1.call-done = bf16[32,3072]{1,0:T(8,128)(2,1)} async-done(((bf16[32,3072]{1,0:T(8,128)(2,1)}), bf16[32,3072]{1,0:T(8,128)(2,1)}) %all-reduce.21.cloned.1.call-update) | async-done | bytes 196624 | tf_op jit(solution)/shard_map/psum | solution.py:65
  474.9 8.4 %multiply_subtract_fusion.7 = f32[32,8,256]{2,0,1:T(8,128)S(1)} fusion(bf16[8,256,3072]{2,1,0:T(8,128)(2,1)} %copy-done.1, f32[32,8,256]{2,0,1:T(8,128)S(1)} %get-tuple-element.50, f32[32,3072]{1,0:T(8,128)S(1)} %get-tuple-element.19, f32[]{:T(128)S(6)} %mul.286, f32[]{:T(128)S(6)} %mul.268, f32[8,256]{1,0:T(8,128)S(1)} %reshape.25, ...), kind=kOutput, calls=%fused_computation.40 | convolution fusion | flops 403668992 | bytes 13770760 | tf_op jit(solution)/shard_map/kmu,tu->tkm/dot_general | solution.py:73
  (73 shorter events, 14.3 us)
Async XLA Ops:
  7.2 109.4 %copy-start = (f32[16384]{0:T(1024)S(1)}, f32[16384]{0:T(1024)}, u32[]{:S(2)}) copy-start(f32[16384]{0:T(1024)} %param.17) | copy-start | bytes 196612
  7.2 139.3 %all-reduce.15.cloned.1.call-start = ((), (), s32[]{:S(2)}) async-start(), calls=%async_computation | async-start | bytes 393216 | tf_op jit(solution)/shard_map/psum | solution.py:65
  14.2 19.3 %copy-start.3 = (f32[32,8,256]{2,1,0:T(8,128)S(1)}, f32[32,8,256]{2,1,0:T(8,128)}, u32[]{:S(2)}) copy-start(f32[32,8,256]{2,1,0:T(8,128)} %param.26) | copy-start | bytes 786436
  45.0 4.6 copy-start.1
  49.6 3.1 copy-start.9
  49.6 3.1 copy-start.6
  49.6 27.6 %copy-start.7 = (f32[2,3072]{1,0:T(2,128)S(1)}, f32[2,3072]{1,0:T(2,128)}, u32[]{:S(2)}) copy-start(f32[2,3072]{1,0:T(2,128)} %param.27) | copy-start | bytes 73732
  49.6 46.5 %copy-start.11 = (s32[8,256]{1,0:T(8,128)S(1)}, s32[8,256]{1,0:T(8,128)}, u32[]{:S(2)}) copy-start(s32[8,256]{1,0:T(8,128)} %param.16) | copy-start | bytes 24580
  49.6 46.6 %copy-start.8 = (f32[2,3072]{1,0:T(2,128)S(1)}, f32[2,3072]{1,0:T(2,128)}, u32[]{:S(2)}) copy-start(f32[2,3072]{1,0:T(2,128)} %param.25) | copy-start | bytes 73732
  49.6 78.8 %copy-start.5 = (f32[3072]{0:T(1024)S(1)}, f32[3072]{0:T(1024)}, u32[]{:S(2)}) copy-start(f32[3072]{0:T(1024)} %param.22) | copy-start | bytes 36868
  49.6 78.8 %copy-start.4 = (f32[3072]{0:T(1024)S(1)}, f32[3072]{0:T(1024)}, u32[]{:S(2)}) copy-start(f32[3072]{0:T(1024)} %param.20) | copy-start | bytes 36868
  49.6 78.8 %copy-start.10 = (f32[3072]{0:T(1024)S(1)}, f32[3072]{0:T(1024)}, u32[]{:S(2)}) copy-start(f32[3072]{0:T(1024)} %param.21) | copy-start | bytes 36868
  49.6 78.8 %copy-start.13 = (u32[32]{0:T(128)S(1)}, u32[32]{0:T(128)}, u32[]{:S(2)}) copy-start(u32[32]{0:T(128)} %constant.69) | copy-start | bytes 388
  49.6 80.0 %copy-start.12 = (f32[2]{0:T(128)S(1)}, f32[2]{0:T(128)}, u32[]{:S(2)}) copy-start(f32[2]{0:T(128)} %param.24) | copy-start | bytes 28
  49.7 98.7 %copy-start.2 = (f32[32,8,256]{2,1,0:T(8,128)S(1)}, f32[32,8,256]{2,1,0:T(8,128)}, u32[]{:S(2)}) copy-start(f32[32,8,256]{2,1,0:T(8,128)} %param.18) | copy-start | bytes 786436
  52.6 202.4 %all-reduce.17.cloned.1.call-start = ((), (), s32[]{:S(2)}) async-start(), calls=%async_computation.1 | async-start | bytes 393216 | tf_op jit(solution)/shard_map/psum | solution.py:65
  165.0 199.3 %all-reduce.19.cloned.1.call-start = ((), (), s32[]{:S(2)}) async-start(), calls=%async_computation.2 | async-start | bytes 393216 | tf_op jit(solution)/shard_map/psum | solution.py:65
  274.3 199.3 %all-reduce.21.cloned.1.call-start = ((), (), s32[]{:S(2)}) async-start(), calls=%async_computation.3 | async-start | bytes 393216 | tf_op jit(solution)/shard_map/psum | solution.py:65
Sparse Core Ops, SparseCore 0:
  52.8 93.6 all-reduce.14
  165.2 89.8 all-reduce.16
  274.5 89.8 all-reduce.18
  383.7 89.8 all-reduce.20
where the time goes:
time: 493 us; the launch traced here: 492 us
  waiting for transfers between devices  182 us (37%)
  blocking collectives  157 us (32%)
  matrix products  61 us (12%)
  local copies, waits for them, and re-layouts  45.1 us (9%)
  other arithmetic  24.1 us (5%)
  between operations  23 us (5%)
    psum x4, waiting for transfers between devices, body(): pulled = lax.psum(own_term.astype(jnp.bfloat16), 'ctg').astype(jnp.float32)  182 us
    psum x2, blocking collectives, body(): flow_sq = lax.psum(jnp.sum((dual_new - flow_dual) ** 2), 'ctg')  62.5 us
    dot_general x4, matrix products, body(): jnp.einsum('kmu,tu->tkm', masked, extended_half, preferred_element_type=j...  35.6 us
    unnamed x1, blocking collectives  31.2 us
    mul x2, local copies, waits for them, and re-layouts, mask_tiles(): return (blocks * gates).reshape(ctg_count, line_count, unit_count)  25.6 us
    dot_general x4, matrix products, body(): jnp.einsum('tkm,kmu->tu', dual_half, masked, preferred_element_type=jnp.f...  25.4 us
    all_gather x1, blocking collectives, body(): lax.all_gather(unit_cost, 'ctg', axis=0, tiled=True)  24.2 us
    all_gather x1, blocking collectives, body(): lax.all_gather(start_output, 'ctg', axis=0, tiled=True)  20.1 us
  transfers between devices with their start and end apart: 4, of which 4 were waited for; matrix products, arithmetic and copies ran while one was open for 3% of the time, Pallas kernels for 0%

commit v1 on v0

v1 whole, which is shorter than its diff:
```python
import functools
import math

import jax
import jax.numpy as jnp
from jax import lax
from jax.experimental import pallas as pl
from jax.experimental.pallas import tpu as pltpu
from jax.sharding import PartitionSpec as P

ITERS = 4
ROWS = 16


def send(src, dst, send_sem, recv_sem, target):
    return pltpu.make_async_remote_copy(
        src_ref=src,
        dst_ref=dst,
        send_sem=send_sem,
        recv_sem=recv_sem,
        device_id={"ctg": target},
        device_id_type=pl.DeviceIdType.MESH,
    )


def kernel(
    n, hour_rows, step_size, balance,
    tiles, gates, index, table, base, start_dual, starts, demand, units,
    out_levels, out_dual, out_ramp, out_price,
    masked, limit, dual_half, flow_acc,
    start_stage, frag_in, frag_out,
    cost, levels, ramp, extended, halo_ext, halo_ramp,
    pull_out, pull_in, ext_half, stats, price, omega,
    tile_sem, frag_send, frag_recv, fin_send, fin_recv,
    pull_send, pull_recv, ext_send, ext_recv, stat_send, stat_recv,
    halo_sems,
):
    f32 = jnp.float32
    bf16 = jnp.bfloat16
    members = ROWS // hour_rows
    groups = n // members
    chunks = n // groups
    unit_count = tiles.shape[2]
    width = unit_count // chunks
    ctgs, lines = tiles.shape[0], tiles.shape[1]
    hours = groups * ROWS
    pairs = chunks // 2

    me = lax.axis_index("ctg")
    my_chunk = lax.div(me, groups)
    my_group = lax.rem(me, groups)
    home_group = lax.div(me, members)
    home_row = lax.rem(me, members)
    my_pair = lax.div(my_chunk, 2)
    my_rows = pl.ds(pl.multiple_of(my_group * ROWS, ROWS), ROWS)
    my_lanes = pl.ds(pl.multiple_of(my_chunk * width, 128), width)

    def tile_copy(k):
        return pltpu.make_async_copy(
            tiles.at[k], masked.at[pl.ds(pl.multiple_of(k * lines, lines), lines)], tile_sem.at[k]
        )

    for k in range(ctgs):
        tile_copy(k).start()

    barrier = pltpu.get_barrier_semaphore()

    @pl.loop(1, n)
    def _(d):
        pl.semaphore_signal(
            barrier, inc=1, device_id={"ctg": lax.rem(me + d, n)}, device_id_type=pl.DeviceIdType.MESH
        )

    pl.semaphore_wait(barrier, n - 1)

    def frag_copy(c, target):
        return send(
            starts.at[:, :, pl.ds(pl.multiple_of(c * width, 128), width)],
            start_stage.at[home_row], frag_send.at[c], frag_recv.at[home_row], target,
        )

    for c in range(chunks):
        target = c * groups + home_group

        @pl.when(target != me)
        def _():
            frag_copy(c, target).start()

        @pl.when(target == me)
        def _():
            start_stage[home_row] = starts[:, :, c * width:(c + 1) * width]

    def stat_copy(slot, target, sender):
        return send(
            stats.at[slot, sender], stats.at[slot, sender],
            stat_send.at[slot % 2, target], stat_recv.at[slot % 2, sender], target,
        )

    def stat_start(slot):
        @pl.loop(1, n)
        def _(d):
            stat_copy(slot, lax.rem(me + d, n), me).start()

    def stat_wait(slot):
        @pl.loop(1, n)
        def _(d):
            peer = lax.rem(me + d, n)
            stat_copy(slot, peer, me).wait_send()
            stat_copy(slot, peer, peer).wait_recv()

    stats[0, me] = demand[...]
    stat_start(0)

    row_iota = lax.broadcasted_iota(jnp.int32, (128, 256), 0)
    values = table[...]
    part_a = values.astype(bf16)
    rest = values - part_a.astype(f32)
    part_b = rest.astype(bf16)
    part_c = (rest - part_b.astype(f32)).astype(bf16)
    for k in range(ctgs * lines // 256):
        which = index[:, k * 256:(k + 1) * 256]
        high = lax.shift_right_logical(which, 7)
        low = lax.bitwise_and(which, 127)
        blocks = table.shape[1] // 128
        got = jnp.zeros((128, 256), f32)
        for b in range(blocks):
            pick = jnp.where(row_iota + b * 128 == high, 1.0, 0.0).astype(bf16)
            for part in (part_a, part_b, part_c):
                got = got + jnp.dot(part[:, b * 128:(b + 1) * 128], pick, preferred_element_type=f32)
        limit[:, k * 256:(k + 1) * 256] = jnp.sum(
            jnp.where(row_iota == low, got, 0.0), axis=0, keepdims=True
        )

    out_dual[...] = start_dual[...]
    dual_half[...] = start_dual[...].astype(bf16)
    omega[...] = jnp.ones_like(omega)
    price[...] = jnp.zeros_like(price)

    @pl.loop(0, ctgs)
    def _(k):
        tile_copy(k).wait()
        for half in range(lines // 128):
            gate = jnp.broadcast_to(gates[k * (lines // 128) + half], (16, unit_count)).astype(bf16)
            for r in range(8):
                where = pl.ds(pl.multiple_of(k * lines + half * 128 + r * 16, 16), 16)
                masked[where, :] = masked[where, :] * gate

    for r in range(members):
        peer = my_group * members + r

        @pl.when(peer != me)
        def _():
            send(
                starts.at[:, :, pl.ds(0, width)], start_stage.at[r],
                frag_send.at[0], frag_recv.at[r], peer,
            ).wait_recv()

    for c in range(chunks):
        target = c * groups + home_group

        @pl.when(target != me)
        def _():
            frag_copy(c, target).wait_send()

    for r in range(members):
        rows = slice(r * hour_rows, (r + 1) * hour_rows)
        levels[rows, :] = start_stage[r, 0]
        cost[rows, :] = start_stage[r, 1]
        ramp[rows, :] = start_stage[r, 2]

    floor = units[0:1, my_lanes]
    ceiling = floor + units[1:2, my_lanes]
    ramp_limit = units[2:3, my_lanes]
    ramp_on = units[3:4, my_lanes]
    block_row = lax.broadcasted_iota(jnp.int32, (ROWS, width), 0)
    lane_here = lax.broadcasted_iota(jnp.int32, (ROWS, 128), 1)
    row_here = lax.broadcasted_iota(jnp.int32, (ROWS, 128), 0) + my_group * ROWS
    diagonal = lane_here == row_here
    hour_lanes = lax.broadcasted_iota(jnp.int32, (1, 128), 1) < hours
    stat_row = lax.broadcasted_iota(jnp.int32, (8, 128), 0)

    def pull_copy(it, c, g, target, sender):
        return send(
            pull_out.at[c, pl.ds(pl.multiple_of(g * ROWS, ROWS), ROWS)], pull_in.at[it, sender],
            pull_send.at[target], pull_recv.at[sender], target,
        )

    def ext_copy(it, target, sender):
        c, g = lax.div(sender, groups), lax.rem(sender, groups)
        spot = ext_half.at[it, c, pl.ds(pl.multiple_of(g * ROWS, ROWS), ROWS)]
        return send(spot, spot, ext_send.at[target], ext_recv.at[sender], target)

    def halo_ext_copy(it, target):
        return send(extended.at[pl.ds(0, 8)], halo_ext.at[it], halo_sems.at[0], halo_sems.at[1], target)

    def halo_ramp_copy(it, target):
        return send(ramp.at[pl.ds(ROWS - 8, 8)], halo_ramp.at[it], halo_sems.at[2], halo_sems.at[3], target)

    def absorb(slot, sigma):
        total = stats[slot, 0]
        for q in range(1, n):
            total = total + stats[slot, q]
        move = sigma * (balance * (total[0:1] - price[1:2]))
        move = jnp.where(hour_lanes, move, 0.0)
        price[0:1] = price[0:1] + move
        return total, jnp.sum(move * move, axis=1, keepdims=True)

    @pl.loop(0, ITERS)
    def _(it):
        @pl.when(my_group < groups - 1)
        def _():
            halo_ramp_copy(it, me + 1).start()

        @pl.loop(0, pairs)
        def _(j):
            pair = lax.rem(my_pair + 1 + j, pairs)
            lanes = pl.ds(pl.multiple_of(pair * (2 * width), 256), 2 * width)
            part = jnp.dot(dual_half[...], masked[:, lanes], preferred_element_type=f32).astype(bf16)
            for side in range(2):
                c = pair * 2 + side
                pull_out[c] = part[:, side * width:(side + 1) * width]
                for g in range(groups):
                    target = c * groups + g

                    @pl.when(target != me)
                    def _():
                        pull_copy(it, c, g, target, me).start()

        pull_in[it, me] = pull_out[my_chunk, my_rows, :]

        stat_wait(it)

        @pl.when(it == 0)
        def _():
            first = stats[0, 0]
            for q in range(1, n):
                first = first + stats[0, q]
            price[1:2] = first[0:1]

        @pl.when(it > 0)
        def _():
            old = omega[0:1, 0:1]
            total, price_sq = absorb(it, step_size * old)
            sums = jnp.sum(total, axis=1, keepdims=True)
            dual_sq = sums[3:4] + sums[2:3] + price_sq
            ratio = (dual_sq + 1e-06) / (sums[1:2] + 1e-06)
            omega[...] = jnp.broadcast_to(jnp.sqrt(old) * jnp.sqrt(jnp.sqrt(ratio)), omega.shape)

        weight = omega[0:1, 0:1]
        tau = step_size / weight
        sigma = step_size * weight

        @pl.loop(1, n)
        def _(d):
            peer = lax.rem(me + d, n)
            pull_copy(it, lax.div(peer, groups), lax.rem(peer, groups), peer, me).wait_send()
            pull_copy(it, 0, 0, peer, peer).wait_recv()

        pulled = pull_in[it, 0].astype(f32)
        for q in range(1, n):
            pulled = pulled + pull_in[it, q].astype(f32)

        @pl.when(my_group < groups - 1)
        def _():
            halo_ramp_copy(it, me + 1).wait_send()

        @pl.when(my_group > 0)
        def _():
            halo_ramp_copy(it, me - 1).wait_recv()

        @pl.when(my_group == 0)
        def _():
            halo_ramp[it] = jnp.zeros_like(halo_ramp[it])

        ramp_now = ramp[...]
        before = jnp.where(block_row == 0, halo_ramp[it][7:8], pltpu.roll(ramp_now, 1, 0))
        price_here = jnp.sum(
            jnp.where(diagonal, jnp.broadcast_to(price[0:1], (ROWS, 128)), 0.0), axis=1, keepdims=True
        )
        gradient = cost[...] + pulled + ramp_on * (before - ramp_now) + balance * price_here
        old_levels = levels[...]
        moved = jnp.clip(old_levels - tau * gradient, floor, ceiling)
        ext = 2.0 * moved - old_levels
        levels[...] = moved
        ext_half[it, my_chunk, my_rows, :] = ext.astype(bf16)
        extended[...] = ext

        @pl.loop(1, n)
        def _(d):
            ext_copy(it, lax.rem(me + d, n), me).start()

        @pl.when(my_group > 0)
        def _():
            halo_ext_copy(it, me - 1).start()
            halo_ext_copy(it, me - 1).wait_send()

        @pl.when(my_group < groups - 1)
        def _():
            halo_ext_copy(it, me + 1).wait_recv()

        @pl.when(my_group == groups - 1)
        def _():
            halo_ext[it] = jnp.zeros_like(halo_ext[it])

        after = jnp.where(block_row == ROWS - 1, halo_ext[it][0:1], pltpu.roll(ext, ROWS - 1, 0))
        change = ramp_on * (after - ext)
        last_hour = block_row + my_group * ROWS == hours - 1
        change = jnp.where(last_hour, 0.0, change)
        trial = ramp_now + sigma * change
        ramp_new = trial - sigma * jnp.clip(trial / sigma, -ramp_limit, ramp_limit)
        ramp[...] = ramp_new

        def lane_sums(x):
            x = jnp.sum(x, axis=0, keepdims=True)
            out = x[:, 0:128]
            for b in range(1, width // 128):
                out = out + x[:, b * 128:(b + 1) * 128]
            return out

        row_sums = jnp.sum(ext, axis=1, keepdims=True)
        row_sums = jnp.sum(
            jnp.where(diagonal, jnp.broadcast_to(row_sums, (ROWS, 128)), 0.0), axis=0, keepdims=True
        )
        primal_sq = lane_sums((moved - old_levels) ** 2)
        ramp_sq = lane_sums((ramp_new - ramp_now) ** 2)
        report = jnp.where(
            stat_row == 0, row_sums,
            jnp.where(stat_row == 1, primal_sq, jnp.where(stat_row == 2, ramp_sq, 0.0)),
        )

        @pl.when(it == ITERS - 1)
        def _():
            stats[it + 1, me] = report
            stat_start(it + 1)
            for r in range(members):
                rows = slice(r * hour_rows, (r + 1) * hour_rows)
                frag_out[r, 0] = moved[rows, :]
                frag_out[r, 1] = ramp_new[rows, :]
            for r in range(members):
                target = my_group * members + r

                @pl.when(target != me)
                def _():
                    send(
                        frag_out.at[r], frag_in.at[my_chunk], fin_send.at[r], fin_recv.at[my_chunk], target
                    ).start()

                @pl.when(target == me)
                def _():
                    frag_in[my_chunk] = frag_out[r]

        @pl.loop(0, pairs)
        def _(j):
            pair = lax.rem(my_pair + j, pairs)
            for side in range(2):
                for g in range(groups):
                    peer = (pair * 2 + side) * groups + g

                    @pl.when(peer != me)
                    def _():
                        ext_copy(it, peer, peer).wait_recv()

            lanes = pl.ds(pl.multiple_of(pair * (2 * width), 256), 2 * width)
            x = jnp.concatenate([ext_half[it, pair * 2], ext_half[it, pair * 2 + 1]], axis=1)
            part = lax.dot_general(
                x, masked[:, lanes], (((1,), (1,)), ((), ())), preferred_element_type=f32
            )

            @pl.when(j == 0)
            def _():
                flow_acc[...] = part

            @pl.when(j > 0)
            def _():
                flow_acc[...] += part

        @pl.loop(1, n)
        def _(d):
            ext_copy(it, lax.rem(me + d, n), me).wait_send()

        old_dual = out_dual[...]
        trial = old_dual + sigma * flow_acc[...]
        bound = limit[...]
        dual_new = trial - sigma * jnp.clip(trial / sigma, base[...] - bound, base[...] + bound)
        out_dual[...] = dual_new
        dual_half[...] = dual_new.astype(bf16)

        @pl.when(it < ITERS - 1)
        def _():
            moved_sq = jnp.sum((dual_new - old_dual) ** 2, axis=0, keepdims=True)
            flow_sq = moved_sq[:, 0:128]
            for b in range(1, ctgs * lines // 128):
                flow_sq = flow_sq + moved_sq[:, b * 128:(b + 1) * 128]
            stats[it + 1, me] = jnp.where(stat_row == 3, flow_sq, report)
            stat_start(it + 1)

    stat_wait(ITERS)
    absorb(ITERS, step_size * omega[0:1, 0:1])
    out_price[...] = price[...]
    for r in range(members):
        target = my_group * members + r

        @pl.when(target != me)
        def _():
            send(
                frag_out.at[r], frag_in.at[my_chunk], fin_send.at[r], fin_recv.at[my_chunk], target
            ).wait_send()

    for c in range(chunks):
        peer = c * groups + home_group

        @pl.when(peer != me)
        def _():
            send(frag_out.at[0], frag_in.at[c], fin_send.at[0], fin_recv.at[c], peer).wait_recv()

    for c in range(chunks):
        out_levels[:, c * width:(c + 1) * width] = frag_in[c, 0]
        out_ramp[:, c * width:(c + 1) * width] = frag_in[c, 1]


def body(
    flow_tiles,
    tile_pattern,
    monitored,
    ratings,
    base_flow,
    unit_cost,
    unit_floor,
    unit_span,
    ramp_limit,
    ramp_mask,
    demand,
    start_output,
    start_flow_dual,
    start_ramp_dual,
):
    f32, bf16 = jnp.float32, jnp.bfloat16
    ctgs, lines, unit_count = flow_tiles.shape
    n = lax.axis_size("ctg")
    position = lax.axis_index("ctg")
    hour_rows = start_output.shape[0]
    hours = hour_rows * n
    groups = hours // ROWS
    chunks = n // groups
    members = ROWS // hour_rows
    width = unit_count // chunks
    flat = ctgs * lines
    step_size = 0.5 / (2.0 + math.sqrt(ctgs * n * lines / unit_count))
    balance = 1.0 / math.sqrt(unit_count)

    gates = jnp.repeat(tile_pattern.astype(f32).reshape(-1, unit_count // 128), 128, axis=1)[:, None, :]
    index = monitored.reshape(1, flat)
    table = ratings.reshape(-1, 128).T
    base = base_flow.reshape(hours, flat)
    start_dual = start_flow_dual.reshape(hours, flat)
    starts = jnp.stack([start_output, unit_cost, start_ramp_dual])
    hour = lax.broadcasted_iota(jnp.int32, (8, 128), 1) - position * hour_rows
    top = lax.broadcasted_iota(jnp.int32, (8, 128), 0) == 0
    own_demand = jnp.zeros((8, 128), f32)
    for r in range(hour_rows):
        own_demand = jnp.where(top & (hour == r), demand[r], own_demand)
    units = jnp.stack([unit_floor, unit_span, ramp_limit, ramp_mask.astype(f32)])

    vmem = pl.BlockSpec(memory_space=pltpu.VMEM)
    sem = pltpu.SemaphoreType.DMA
    out = pl.pallas_call(
        functools.partial(kernel, n, hour_rows, step_size, balance),
        out_shape=(
            jax.ShapeDtypeStruct((hour_rows, unit_count), f32),
            jax.ShapeDtypeStruct((hours, flat), f32),
            jax.ShapeDtypeStruct((hour_rows, unit_count), f32),
            jax.ShapeDtypeStruct((8, 128), f32),
        ),
        in_specs=[pl.BlockSpec(memory_space=pl.ANY)] + [vmem] * 8,
        out_specs=(vmem,) * 4,
        scratch_shapes=[
            pltpu.VMEM((flat, unit_count), bf16),
            pltpu.VMEM((1, flat), f32),
            pltpu.VMEM((hours, flat), bf16),
            pltpu.VMEM((hours, flat), f32),
            pltpu.VMEM((members, 3, hour_rows, width), f32),
            pltpu.VMEM((chunks, 2, hour_rows, width), f32),
            pltpu.VMEM((members, 2, hour_rows, width), f32),
            pltpu.VMEM((ROWS, width), f32),
            pltpu.VMEM((ROWS, width), f32),
            pltpu.VMEM((ROWS, width), f32),
            pltpu.VMEM((ROWS, width), f32),
            pltpu.VMEM((ITERS, 8, width), f32),
            pltpu.VMEM((ITERS, 8, width), f32),
            pltpu.VMEM((chunks, hours, width), bf16),
            pltpu.VMEM((ITERS, n, ROWS, width), bf16),
            pltpu.VMEM((ITERS, chunks, hours, width), bf16),
            pltpu.VMEM((ITERS + 1, n, 8, 128), f32),
            pltpu.VMEM((8, 128), f32),
            pltpu.VMEM((8, 128), f32),
            sem((ctgs,)),
            sem((chunks,)), sem((members,)), sem((members,)), sem((chunks,)),
            sem((n,)), sem((n,)), sem((n,)), sem((n,)), sem((2, n)), sem((2, n)),
            sem((4,)),
        ],
        compiler_params=pltpu.CompilerParams(collective_id=0, has_side_effects=True),
    )(flow_tiles, gates, index, table, base, start_dual, starts, own_demand, units)
    own_levels, flow_dual, own_ramp, price = out
    own_price = lax.dynamic_slice_in_dim(price[0], position * hour_rows, hour_rows, 0)
    return (own_levels, flow_dual.reshape(hours, ctgs, lines), own_ramp, own_price)


def solution(mesh):
    return jax.shard_map(
        body,
        mesh=mesh,
        in_specs=(
            P("ctg", None, None),
            P("ctg", None, None),
            P("ctg", None),
            P(),
            P("grp", "ctg", None),
            P(("grp", "ctg"), None),
            P(),
            P(),
            P(),
            P(),
            P(("grp", "ctg")),
            P(("grp", "ctg"), None),
            P("grp", "ctg", None),
            P(("grp", "ctg"), None),
        ),
        out_specs=(
            P(("grp", "ctg"), None),
            P("grp", "ctg", None),
            P(("grp", "ctg"), None),
            P(("grp", "ctg")),
        ),
        check_vma=False,
    )
```

time: 493 us -> 102 us (0.21)
  waiting for transfers between devices: 182 us -> 0 us
  blocking collectives: 157 us -> 0 us
  Pallas kernels: 0 us -> 79.8 us
  matrix products: 61 us -> 0 us
  local copies, waits for them, and re-layouts: 45.1 us -> 14.1 us
  between operations: 23 us -> 0.66 us
  other arithmetic: 24.1 us -> 6.21 us
    psum x4 -> x0, waiting for transfers between devices: 182 us -> none  [body(): pulled = lax.psum(own_term.astype(jnp.bfloat16), 'ctg').astype(jnp.float32)]
    pallas_call x0 -> x1, Pallas kernels: none -> 79.8 us  [body(): pl.pallas_call(functools.partial(kernel, n, hour_rows, step_size, balance...]
    all_gather x3 -> x0, blocking collectives: 62.9 us -> none  [the longest x1 24.2 us: body(): lax.all_gather(unit_cost, 'ctg', axis=0, tiled=True)]
    psum x2 -> x0, blocking collectives: 62.5 us -> none  [body(): flow_sq = lax.psum(jnp.sum((dual_new - flow_dual) ** 2), 'ctg')]
    dot_general x8 -> x0, matrix products: 61 us -> none  [the longest x4 35.6 us: body(): jnp.einsum('kmu,tu->tkm', masked, extended_half, preferred_element_type=j...]
    unnamed x1 -> x0, blocking collectives: 31.2 us -> none
    mul x2 -> x0, local copies, waits for them, and re-layouts: 25.6 us -> none  [mask_tiles(): return (blocks * gates).reshape(ctg_count, line_count, unit_count)]
    gather x2 -> x0, local copies, waits for them, and re-layouts: 11.8 us -> none  [body(): flow_limit = ratings[monitored]]
  transfers between devices with their start and end apart: 4 -> 0, of which waited for: 4 -> 0; matrix products, arithmetic and copies ran while one was open for 3% -> 0% of each run, Pallas kernels for 0% -> 0%
where the time goes in v1:
time: 102 us; the launch traced here: 101 us
  Pallas kernels  79.8 us (78%)
  local copies, waits for them, and re-layouts  14.1 us (14%)
  other arithmetic  6.21 us (6%)
    pallas_call x1, Pallas kernels, body(): pl.pallas_call(functools.partial(kernel, n, hour_rows, step_size, balance...  79.8 us
    unnamed x6, local copies, waits for them, and re-layouts  9.19 us

profile of v1, /device:TPU:0, one launch (start us, length us, event | category | flops | bytes accessed | tf_op | source)
XLA Modules:
  0.0 100.7 jit_solution(15976380134045255952)
XLA Ops:
  0.7 1.3 %fusion.2 = (f32[1]{0:T(128)}, f32[1]{0:T(128)}) fusion(f32[2]{0:T(128)} %param.24), kind=kLoop, calls=%fused_computation.8 | loop fusion | bytes 16 | tf_op jit(solution)/shard_map/slice | solution.py:461
  2.0 2.0 %select_select_fusion.demand = f32[8,128]{1,0:T(8,128)} fusion(f32[]{:T(128)} %bitcast.8, f32[]{:T(128)} %bitcast.7, pred[128]{0:T(512)(128)(4,1)S(1)} %get-tuple-element.14, pred[128]{0:T(512)(128)(4,1)S(1)} %get-tuple-element.15, pred[8]{0:T(512)(128)(4,1)S(1)} %iota_compare_fusion), kind=kLoop, calls=%fused_computation.2 | loop fusion | flops 4096 | bytes 4368 | tf_op jit(solution)/shard_map/jit(_where)/select_n | solution.py:461
  3.9 0.7 convert_element_type.6
  4.6 1.3 %copy.19 = s32[1,1,8,256]{3,1,2,0:T(1,128)} copy(s32[1,1,8,256]{3,2,1,0:T(8,128)} %bitcast.42) | data formatting | bytes 16384
  5.9 0.7 convert_element_type.7
  6.6 1.4 %pad_maximum_fusion.1.units = f32[4,3072]{1,0:T(4,128)} fusion(f32[1,3072]{1,0:T(1,128)S(1)} %bitcast.33, f32[1,3072]{1,0:T(1,128)} %bitcast.39, f32[1,3072]{1,0:T(1,128)} %bitcast.40, f32[1,3072]{1,0:T(1,128)} %bitcast.41), kind=kLoop, calls=%fused_computation.1 | loop fusion | flops 36864 | bytes 98304 | tf_op jit(solution)/shard_map/stack | solution.py:462
  8.1 1.6 %copy.18 = f32[128,128]{0,1:T(8,128)} copy(f32[128,128]{1,0:T(8,128)} %bitcast.32) | data formatting | bytes 131072 | tf_op jit(solution)/shard_map/reshape | solution.py:453
  9.6 1.4 %pad_maximum_fusion.starts = f32[3,2,3072]{2,1,0:T(2,128)} fusion(f32[1,2,3072]{2,1,0:T(2,128)} %bitcast.36, f32[1,2,3072]{2,1,0:T(2,128)} %bitcast.37, f32[1,2,3072]{2,1,0:T(2,128)} %bitcast.38), kind=kLoop, calls=%fused_computation | loop fusion | flops 36864 | bytes 147456 | tf_op jit(solution)/shard_map/stack | solution.py:456
  11.0 0.8 broadcast_in_dim.13
  11.8 1.7 %copy.20 = f32[4,8,8,256]{3,1,2,0:T(8,128)} copy(f32[4,8,8,256]{3,2,1,0:T(8,128)} %bitcast.28) | data formatting | bytes 524288
  13.6 1.7 %copy.21 = f32[4,8,8,256]{3,1,2,0:T(8,128)} copy(f32[4,8,8,256]{3,2,1,0:T(8,128)} %bitcast.29) | data formatting | bytes 524288
  15.3 79.8 %shard_map.165 = (f32[2,3072]{1,0:T(2,128)}, f32[32,2048]{1,0:T(8,128)}, f32[2,3072]{1,0:T(2,128)}, f32[8,128]{1,0:T(8,128)}) custom-call(bf16[8,256,3072]{2,1,0:T(8,128)(2,1)} %tiles.1, f32[16,1,3072]{2,1,0:T(1,128)} %bitcast.26, s32[1,2048]{1,0:T(1,128)} %bitcast.34, f32[128,128]{1,0:T(8,128)} %bitcast.27, f32[32,2048]{1,0:T(8,128)} %bitcast.24, ...), custom_call_target="tpu_custom_call" | custom-call | tf_op jit(solution)/shard_map/pallas_call | solution.py:466
  95.1 1.7 %copy.22 = f32[4,8,8,256]{3,2,1,0:T(8,128)} copy(f32[4,8,8,256]{3,1,2,0:T(8,128)} %bitcast.31) | data formatting | bytes 524288
  96.8 0.7 slice.11
  97.5 0.6 dynamic-slice_bitcast_fusion
  98.0 1.3 %copy.25 = f32[2,3072]{1,0:T(2,128)} copy(f32[2,3072]{1,0:T(2,128)} %get-tuple-element.20) | data formatting | bytes 49152
  99.4 1.3 %copy.26 = f32[2,3072]{1,0:T(2,128)} copy(f32[2,3072]{1,0:T(2,128)} %get-tuple-element.22) | data formatting | bytes 49152
  (2 shorter events, 0.0 us)

commit v2 on v1

--- a/solution.py
+++ b/solution.py
@@ -25,9 +25,10 @@
 
 def kernel(
     n, hour_rows, step_size, balance,
-    tiles, gates, index, table, base, start_dual, starts, demand, units,
+    tiles, pattern, index, table, base_in, dual_in, level_in, cost_in, ramp_in, demand,
+    floor_in, span_in, ramp_limit_in, ramp_mask_in,
     out_levels, out_dual, out_ramp, out_price,
-    masked, limit, dual_half, flow_acc,
+    masked, base, starts, limit, dual_half, flow_acc,
     start_stage, frag_in, frag_out,
     cost, levels, ramp, extended, halo_ext, halo_ramp,
     pull_out, pull_in, ext_half, stats, price, omega,
@@ -79,6 +80,9 @@
             start_stage.at[home_row], frag_send.at[c], frag_recv.at[home_row], target,
         )
 
+    starts[0] = level_in[...]
+    starts[1] = cost_in[...]
+    starts[2] = ramp_in[...]
     for c in range(chunks):
         target = c * groups + home_group
 
@@ -108,39 +112,53 @@
             stat_copy(slot, peer, me).wait_send()
             stat_copy(slot, peer, peer).wait_recv()
 
-    stats[0, me] = demand[...]
+    hour = lax.broadcasted_iota(jnp.int32, (8, 128), 1) - me * hour_rows
+    own_demand = jnp.zeros((8, 128), f32)
+    for r in range(hour_rows):
+        own_demand = jnp.where(hour == r, demand[r], own_demand)
+    stats[0, me] = own_demand
     stat_start(0)
 
-    row_iota = lax.broadcasted_iota(jnp.int32, (128, 256), 0)
-    values = table[...]
+    row_iota = lax.broadcasted_iota(jnp.int32, (128, lines), 0)
+    values = table[...].T
     part_a = values.astype(bf16)
     rest = values - part_a.astype(f32)
     part_b = rest.astype(bf16)
     part_c = (rest - part_b.astype(f32)).astype(bf16)
-    for k in range(ctgs * lines // 256):
-        which = index[:, k * 256:(k + 1) * 256]
+    for k in range(ctgs):
+        which = index[k:k + 1, :]
         high = lax.shift_right_logical(which, 7)
         low = lax.bitwise_and(which, 127)
-        blocks = table.shape[1] // 128
-        got = jnp.zeros((128, 256), f32)
+        blocks = table.shape[0] // 128
+        got = jnp.zeros((128, lines), f32)
         for b in range(blocks):
             pick = jnp.where(row_iota + b * 128 == high, 1.0, 0.0).astype(bf16)
             for part in (part_a, part_b, part_c):
                 got = got + jnp.dot(part[:, b * 128:(b + 1) * 128], pick, preferred_element_type=f32)
-        limit[:, k * 256:(k + 1) * 256] = jnp.sum(
+        limit[:, k * lines:(k + 1) * lines] = jnp.sum(
             jnp.where(row_iota == low, got, 0.0), axis=0, keepdims=True
         )
 
-    out_dual[...] = start_dual[...]
-    dual_half[...] = start_dual[...].astype(bf16)
+    for k in range(ctgs):
+        lanes = slice(k * lines, (k + 1) * lines)
+        base[:, lanes] = base_in[:, k, :]
+        dual = dual_in[:, k, :]
+        out_dual[:, lanes] = dual
+        dual_half[:, lanes] = dual.astype(bf16)
     omega[...] = jnp.ones_like(omega)
     price[...] = jnp.zeros_like(price)
+
+    tile_count = unit_count // 128
+    tile_row = lax.broadcasted_iota(jnp.int32, (tile_count, unit_count), 0)
+    tile_lane = lax.broadcasted_iota(jnp.int32, (tile_count, unit_count), 1)
+    spread = jnp.where(lax.shift_right_logical(tile_lane, 7) == tile_row, 1.0, 0.0)
 
     @pl.loop(0, ctgs)
     def _(k):
         tile_copy(k).wait()
+        gates = jnp.dot(pattern[k].astype(f32), spread, preferred_element_type=f32)
         for half in range(lines // 128):
-            gate = jnp.broadcast_to(gates[k * (lines // 128) + half], (16, unit_count)).astype(bf16)
+            gate = jnp.broadcast_to(gates[half:half + 1], (16, unit_count)).astype(bf16)
             for r in range(8):
                 where = pl.ds(pl.multiple_of(k * lines + half * 128 + r * 16, 16), 16)
                 masked[where, :] = masked[where, :] * gate
@@ -168,10 +186,10 @@
         cost[rows, :] = start_stage[r, 1]
         ramp[rows, :] = start_stage[r, 2]
 
-    floor = units[0:1, my_lanes]
-    ceiling = floor + units[1:2, my_lanes]
-    ramp_limit = units[2:3, my_lanes]
-    ramp_on = units[3:4, my_lanes]
+    floor = floor_in[:, my_lanes]
+    ceiling = floor + span_in[:, my_lanes]
+    ramp_limit = ramp_limit_in[:, my_lanes]
+    ramp_on = ramp_mask_in[:, my_lanes].astype(f32)
     block_row = lax.broadcasted_iota(jnp.int32, (ROWS, width), 0)
     lane_here = lax.broadcasted_iota(jnp.int32, (ROWS, 128), 1)
     row_here = lax.broadcasted_iota(jnp.int32, (ROWS, 128), 0) + my_group * ROWS
@@ -416,6 +434,18 @@
     for c in range(chunks):
         out_levels[:, c * width:(c + 1) * width] = frag_in[c, 0]
         out_ramp[:, c * width:(c + 1) * width] = frag_in[c, 1]
+
+
+def finish(levels, dual, ramp, price, out_levels, out_dual, out_ramp, out_price):
+    lines = out_dual.shape[2]
+    out_levels[...] = levels[...]
+    out_ramp[...] = ramp[...]
+    for k in range(out_dual.shape[1]):
+        out_dual[:, k, :] = dual[:, k * lines:(k + 1) * lines]
+    hour_rows = out_price.shape[0]
+    lane = lax.broadcasted_iota(jnp.int32, (1, 128), 1) - lax.axis_index("ctg") * hour_rows
+    for r in range(hour_rows):
+        out_price[r] = jnp.sum(jnp.where(lane == r, price[0:1], 0.0))
 
 
 def body(
@@ -437,7 +467,6 @@
     f32, bf16 = jnp.float32, jnp.bfloat16
     ctgs, lines, unit_count = flow_tiles.shape
     n = lax.axis_size("ctg")
-    position = lax.axis_index("ctg")
     hour_rows = start_output.shape[0]
     hours = hour_rows * n
     groups = hours // ROWS
@@ -447,19 +476,6 @@
     flat = ctgs * lines
     step_size = 0.5 / (2.0 + math.sqrt(ctgs * n * lines / unit_count))
     balance = 1.0 / math.sqrt(unit_count)
-
-    gates = jnp.repeat(tile_pattern.astype(f32).reshape(-1, unit_count // 128), 128, axis=1)[:, None, :]
-    index = monitored.reshape(1, flat)
-    table = ratings.reshape(-1, 128).T
-    base = base_flow.reshape(hours, flat)
-    start_dual = start_flow_dual.reshape(hours, flat)
-    starts = jnp.stack([start_output, unit_cost, start_ramp_dual])
-    hour = lax.broadcasted_iota(jnp.int32, (8, 128), 1) - position * hour_rows
-    top = lax.broadcasted_iota(jnp.int32, (8, 128), 0) == 0
-    own_demand = jnp.zeros((8, 128), f32)
-    for r in range(hour_rows):
-        own_demand = jnp.where(top & (hour == r), demand[r], own_demand)
-    units = jnp.stack([unit_floor, unit_span, ramp_limit, ramp_mask.astype(f32)])
 
     vmem = pl.BlockSpec(memory_space=pltpu.VMEM)
     sem = pltpu.SemaphoreType.DMA
@@ -471,10 +487,15 @@
             jax.ShapeDtypeStruct((hour_rows, unit_count), f32),
             jax.ShapeDtypeStruct((8, 128), f32),
         ),
-        in_specs=[pl.BlockSpec(memory_space=pl.ANY)] + [vmem] * 8,
+        in_specs=[pl.BlockSpec(memory_space=pl.ANY)]
+        + [vmem] * 8
+        + [pl.BlockSpec(memory_space=pltpu.SMEM)]
+        + [vmem] * 4,
         out_specs=(vmem,) * 4,
         scratch_shapes=[
             pltpu.VMEM((flat, unit_count), bf16),
+            pltpu.VMEM((hours, flat), f32),
+            pltpu.VMEM((3, hour_rows, unit_count), f32),
             pltpu.VMEM((1, flat), f32),
             pltpu.VMEM((hours, flat), bf16),
             pltpu.VMEM((hours, flat), f32),
@@ -499,10 +520,33 @@
             sem((4,)),
         ],
         compiler_params=pltpu.CompilerParams(collective_id=0, has_side_effects=True),
-    )(flow_tiles, gates, index, table, base, start_dual, starts, own_demand, units)
-    own_levels, flow_dual, own_ramp, price = out
-    own_price = lax.dynamic_slice_in_dim(price[0], position * hour_rows, hour_rows, 0)
-    return (own_levels, flow_dual.reshape(hours, ctgs, lines), own_ramp, own_price)
+    )(
+        flow_tiles,
+        tile_pattern,
+        monitored,
+        ratings.reshape(-1, 128),
+        base_flow,
+        start_flow_dual,
+        start_output,
+        unit_cost,
+        start_ramp_dual,
+        demand,
+        unit_floor[None],
+        unit_span[None],
+        ramp_limit[None],
+        ramp_mask[None],
+    )
+    return pl.pallas_call(
+        finish,
+        out_shape=(
+            jax.ShapeDtypeStruct((hour_rows, unit_count), f32),
+            jax.ShapeDtypeStruct((hours, ctgs, lines), f32),
+            jax.ShapeDtypeStruct((hour_rows, unit_count), f32),
+            jax.ShapeDtypeStruct((hour_rows,), f32),
+        ),
+        in_specs=[vmem] * 4,
+        out_specs=(vmem,) * 3 + (pl.BlockSpec(memory_space=pltpu.SMEM),),
+    )(*out)
 
 
 def solution(mesh):

time: 102 us -> 82.6 us (0.81)
  local copies, waits for them, and re-layouts: 14.1 us -> 0 us
  other arithmetic: 6.21 us -> 0 us
  Pallas kernels: 79.8 us -> 81.6 us
    unnamed x6 -> x0, local copies, waits for them, and re-layouts: 9.19 us -> none
    another operation x2 -> x0, other arithmetic: 2.83 us -> none  [the longest x1 1.42 us: body(): starts = jnp.stack([start_output, unit_cost, start_ramp_dual])]
    slice x2 -> x0, local copies, waits for them, and re-layouts: 1.99 us -> none  [the longest x1 1.31 us: body(): own_demand = jnp.where(top & (hour == r), demand[r], own_demand)]
    select_n x1 -> x0, other arithmetic: 1.96 us -> none  [body(): own_demand = jnp.where(top & (hour == r), demand[r], own_demand)]
    pallas_call x0 -> x1, Pallas kernels: none -> 1.76 us  [body(): pl.pallas_call(finish, out_shape=(jax.ShapeDtypeStruct((hour_rows, unit_c...]
    reshape x1 -> x0, local copies, waits for them, and re-layouts: 1.56 us -> none  [body(): table = ratings.reshape(-1, 128).T]
    convert_element_type x2 -> x0, other arithmetic: 1.41 us -> none  [the longest x1 0.71 us: body(): ramp_mask.astype(f32)]
where the time goes in v2:
time: 82.6 us; the launch traced here: 82.3 us
  Pallas kernels  81.6 us (99%)
    pallas_call x1, Pallas kernels, body(): pl.pallas_call(functools.partial(kernel, n, hour_rows, step_size, balance...  79.9 us
    pallas_call x1, Pallas kernels, body(): pl.pallas_call(finish, out_shape=(jax.ShapeDtypeStruct((hour_rows, unit_c...  1.76 us

profile of v2, /device:TPU:0, one launch (start us, length us, event | category | flops | bytes accessed | tf_op | source)
XLA Modules:
  0.0 82.3 jit_solution(12701526529187944922)
XLA Ops:
  0.6 79.9 %shard_map.165 = (f32[2,3072]{1,0:T(2,128)}, f32[32,2048]{1,0:T(8,128)}, f32[2,3072]{1,0:T(2,128)}, f32[8,128]{1,0:T(8,128)}) custom-call(bf16[8,256,3072]{2,1,0:T(8,128)(2,1)} %tiles.1, s32[8,2,24]{2,1,0:T(2,128)} %pattern.1, s32[8,256]{1,0:T(8,128)} %index.1, f32[128,128]{1,0:T(8,128)} %bitcast.5, f32[32,8,256]{2,1,0:T(8,128)} %base_in.1, ...), custom_call_target="tpu_custom_call" | custom-call | tf_op jit(solution)/shard_map/pallas_call | solution.py:482
  80.5 1.8 %shard_map.166 = (f32[2,3072]{1,0:T(2,128)}, f32[32,8,256]{2,1,0:T(8,128)}, f32[2,3072]{1,0:T(2,128)}, f32[2]{0:T(128)}) custom-call(f32[2,3072]{1,0:T(2,128)} %get-tuple-element.8.levels, f32[32,2048]{1,0:T(8,128)} %get-tuple-element.9.dual, f32[2,3072]{1,0:T(2,128)} %get-tuple-element.10.ramp, f32[8,128]{1,0:T(8,128)} %get-tuple-element.11.price), custom_call_target="tpu_custom_call" | custom-call | tf_op jit(solution)/shard_map/pallas_call | solution.py:539

commit v3 on v2

--- a/solution.py
+++ b/solution.py
@@ -31,9 +31,9 @@
     masked, base, starts, limit, dual_half, flow_acc,
     start_stage, frag_in, frag_out,
     cost, levels, ramp, extended, halo_ext, halo_ramp,
-    pull_out, pull_in, ext_half, stats, price, omega,
+    pull_out, pair_in, pull_sum, pull_in, ext_half, stats, price, omega,
     tile_sem, frag_send, frag_recv, fin_send, fin_recv,
-    pull_send, pull_recv, ext_send, ext_recv, stat_send, stat_recv,
+    pair_send, pair_recv, pull_send, pull_recv, ext_send, ext_recv, pass_send, stat_send, stat_recv,
     halo_sems,
 ):
     f32 = jnp.float32
@@ -53,6 +53,10 @@
     home_group = lax.div(me, members)
     home_row = lax.rem(me, members)
     my_pair = lax.div(my_chunk, 2)
+    core = lax.rem(me, 2)
+    chip = lax.div(me, 2)
+    partner = me + 1 - 2 * core
+    chips = n // 2
     my_rows = pl.ds(pl.multiple_of(my_group * ROWS, ROWS), ROWS)
     my_lanes = pl.ds(pl.multiple_of(my_chunk * width, 128), width)
 
@@ -197,16 +201,33 @@
     hour_lanes = lax.broadcasted_iota(jnp.int32, (1, 128), 1) < hours
     stat_row = lax.broadcasted_iota(jnp.int32, (8, 128), 0)
 
-    def pull_copy(it, c, g, target, sender):
+    def block_rows(g):
+        return pl.ds(pl.multiple_of(g * ROWS, ROWS), ROWS)
+
+    def pair_copy(it, owner):
+        c, g = lax.div(owner, groups), lax.rem(owner, groups)
         return send(
-            pull_out.at[c, pl.ds(pl.multiple_of(g * ROWS, ROWS), ROWS)], pull_in.at[it, sender],
-            pull_send.at[target], pull_recv.at[sender], target,
-        )
-
-    def ext_copy(it, target, sender):
-        c, g = lax.div(sender, groups), lax.rem(sender, groups)
-        spot = ext_half.at[it, c, pl.ds(pl.multiple_of(g * ROWS, ROWS), ROWS)]
-        return send(spot, spot, ext_send.at[target], ext_recv.at[sender], target)
+            pull_out.at[c, block_rows(g)], pair_in.at[it, c, block_rows(g)],
+            pair_send.at[owner], pair_recv.at[owner], partner,
+        )
+
+    def pull_copy(it, target, sender_chip):
+        c, g = lax.div(target, groups), lax.rem(target, groups)
+        return send(
+            pull_sum.at[c, block_rows(g)], pull_in.at[it, sender_chip],
+            pull_send.at[target], pull_recv.at[sender_chip], target,
+        )
+
+    def ext_copy(it, target, origin, send_sem):
+        c, g = lax.div(origin, groups), lax.rem(origin, groups)
+        spot = ext_half.at[it, c, block_rows(g)]
+        return send(spot, spot, send_sem, ext_recv.at[origin], target)
+
+    def ext_out(it, target):
+        return ext_copy(it, target, me, ext_send.at[target])
+
+    def ext_forward(it, origin):
+        return ext_copy(it, partner, origin, pass_send.at[origin])
 
     def halo_ext_copy(it, target):
         return send(extended.at[pl.ds(0, 8)], halo_ext.at[it], halo_sems.at[0], halo_sems.at[1], target)
@@ -229,22 +250,41 @@
         def _():
             halo_ramp_copy(it, me + 1).start()
 
-        @pl.loop(0, pairs)
+        @pl.loop(0, pairs + 1)
         def _(j):
-            pair = lax.rem(my_pair + 1 + j, pairs)
-            lanes = pl.ds(pl.multiple_of(pair * (2 * width), 256), 2 * width)
-            part = jnp.dot(dual_half[...], masked[:, lanes], preferred_element_type=f32).astype(bf16)
-            for side in range(2):
-                c = pair * 2 + side
-                pull_out[c] = part[:, side * width:(side + 1) * width]
-                for g in range(groups):
-                    target = c * groups + g
-
-                    @pl.when(target != me)
-                    def _():
-                        pull_copy(it, c, g, target, me).start()
-
-        pull_in[it, me] = pull_out[my_chunk, my_rows, :]
+            @pl.when(j < pairs)
+            def _():
+                pair = lax.rem(my_pair + 1 + j, pairs)
+                lanes = pl.ds(pl.multiple_of(pair * (2 * width), 256), 2 * width)
+                part = jnp.dot(dual_half[...], masked[:, lanes], preferred_element_type=f32).astype(bf16)
+                for side in range(2):
+                    c = pair * 2 + side
+                    pull_out[c] = part[:, side * width:(side + 1) * width]
+                    for h in range(groups // 2):
+                        pair_copy(it, c * groups + 2 * h + 1 - core).start()
+
+            @pl.when(j > 0)
+            def _():
+                pair = lax.rem(my_pair + j, pairs)
+                for side in range(2):
+                    c = pair * 2 + side
+                    for h in range(groups // 2):
+                        g = 2 * h + core
+                        target = c * groups + g
+                        pair_copy(it, target).wait_recv()
+                        both = (
+                            pull_out[c, block_rows(g), :].astype(f32)
+                            + pair_in[it, c, block_rows(g), :].astype(f32)
+                        ).astype(bf16)
+
+                        @pl.when(target != me)
+                        def _():
+                            pull_sum[c, block_rows(g), :] = both
+                            pull_copy(it, target, chip).start()
+
+                        @pl.when(target == me)
+                        def _():
+                            pull_in[it, chip] = both
 
         stat_wait(it)
 
@@ -268,14 +308,18 @@
         tau = step_size / weight
         sigma = step_size * weight
 
-        @pl.loop(1, n)
+        @pl.loop(1, chips)
         def _(d):
-            peer = lax.rem(me + d, n)
-            pull_copy(it, lax.div(peer, groups), lax.rem(peer, groups), peer, me).wait_send()
-            pull_copy(it, 0, 0, peer, peer).wait_recv()
+            other = lax.rem(chip + d, chips)
+            pull_copy(it, other * 2 + core, chip).wait_send()
+            pull_copy(it, other * 2 + core, other).wait_recv()
+
+        @pl.loop(0, chips)
+        def _(q):
+            pair_copy(it, q * 2 + 1 - core).wait_send()
 
         pulled = pull_in[it, 0].astype(f32)
-        for q in range(1, n):
+        for q in range(1, chips):
             pulled = pulled + pull_in[it, q].astype(f32)
 
         @pl.when(my_group < groups - 1)
@@ -303,9 +347,11 @@
         ext_half[it, my_chunk, my_rows, :] = ext.astype(bf16)
         extended[...] = ext
 
-        @pl.loop(1, n)
+        @pl.loop(1, chips)
         def _(d):
-            ext_copy(it, lax.rem(me + d, n), me).start()
+            ext_out(it, lax.rem(chip + d, chips) * 2 + core).start()
+
+        ext_out(it, partner).start()
 
         @pl.when(my_group > 0)
         def _():
@@ -367,17 +413,33 @@
                 def _():
                     frag_in[my_chunk] = frag_out[r]
 
+        def blocks_of(pair, kind, act):
+            for side in range(2):
+                for h in range(groups // 2):
+                    origin = (pair * 2 + side) * groups + 2 * h + kind
+
+                    @pl.when(origin != me)
+                    def _():
+                        act(origin)
+
+        def pass_on(origin):
+            ext_copy(it, partner, origin, pass_send.at[origin]).wait_recv()
+            ext_forward(it, origin).start()
+
+        def take(origin):
+            ext_copy(it, partner, origin, pass_send.at[origin]).wait_recv()
+
+        blocks_of(my_pair, core, pass_on)
+
         @pl.loop(0, pairs)
         def _(j):
             pair = lax.rem(my_pair + j, pairs)
-            for side in range(2):
-                for g in range(groups):
-                    peer = (pair * 2 + side) * groups + g
-
-                    @pl.when(peer != me)
-                    def _():
-                        ext_copy(it, peer, peer).wait_recv()
-
+
+            @pl.when(j < pairs - 1)
+            def _():
+                blocks_of(lax.rem(my_pair + j + 1, pairs), core, pass_on)
+
+            blocks_of(pair, 1 - core, take)
             lanes = pl.ds(pl.multiple_of(pair * (2 * width), 256), 2 * width)
             x = jnp.concatenate([ext_half[it, pair * 2], ext_half[it, pair * 2 + 1]], axis=1)
             part = lax.dot_general(
@@ -392,9 +454,13 @@
             def _():
                 flow_acc[...] += part
 
-        @pl.loop(1, n)
+        @pl.loop(1, chips)
         def _(d):
-            ext_copy(it, lax.rem(me + d, n), me).wait_send()
+            other = lax.rem(chip + d, chips) * 2 + core
+            ext_out(it, other).wait_send()
+            ext_forward(it, other).wait_send()
+
+        ext_out(it, partner).wait_send()
 
         old_dual = out_dual[...]
         trial = old_dual + sigma * flow_acc[...]
@@ -509,14 +575,17 @@
             pltpu.VMEM((ITERS, 8, width), f32),
             pltpu.VMEM((ITERS, 8, width), f32),
             pltpu.VMEM((chunks, hours, width), bf16),
-            pltpu.VMEM((ITERS, n, ROWS, width), bf16),
+            pltpu.VMEM((ITERS, chunks, hours, width), bf16),
+            pltpu.VMEM((chunks, hours, width), bf16),
+            pltpu.VMEM((ITERS, n // 2, ROWS, width), bf16),
             pltpu.VMEM((ITERS, chunks, hours, width), bf16),
             pltpu.VMEM((ITERS + 1, n, 8, 128), f32),
             pltpu.VMEM((8, 128), f32),
             pltpu.VMEM((8, 128), f32),
             sem((ctgs,)),
             sem((chunks,)), sem((members,)), sem((members,)), sem((chunks,)),
-            sem((n,)), sem((n,)), sem((n,)), sem((n,)), sem((2, n)), sem((2, n)),
+            sem((n,)), sem((n,)), sem((n,)), sem((n // 2,)), sem((n,)), sem((n,)), sem((n,)),
+            sem((2, n)), sem((2, n)),
             sem((4,)),
         ],
         compiler_params=pltpu.CompilerParams(collective_id=0, has_side_effects=True),

time: 82.6 us -> 79.7 us (0.965)
  Pallas kernels: 81.6 us -> 78.9 us
    pallas_call x1, Pallas kernels: 79.9 us -> 77.1 us  [body(): pl.pallas_call(functools.partial(kernel, n, hour_rows, step_size, balance...]
where the time goes in v3:
time: 79.7 us; the launch traced here: 79.5 us
  Pallas kernels  78.9 us (99%)
    pallas_call x1, Pallas kernels, body(): pl.pallas_call(functools.partial(kernel, n, hour_rows, step_size, balance...  77.1 us
    pallas_call x1, Pallas kernels, body(): pl.pallas_call(finish, out_shape=(jax.ShapeDtypeStruct((hour_rows, unit_c...  1.76 us

profile of v3, /device:TPU:0, one launch (start us, length us, event | category | flops | bytes accessed | tf_op | source)
XLA Modules:
  0.0 79.5 jit_solution(13845831583060525768)
XLA Ops:
  0.6 77.1 %shard_map.165 = (f32[2,3072]{1,0:T(2,128)}, f32[32,2048]{1,0:T(8,128)}, f32[2,3072]{1,0:T(2,128)}, f32[8,128]{1,0:T(8,128)}) custom-call(bf16[8,256,3072]{2,1,0:T(8,128)(2,1)} %tiles.1, s32[8,2,24]{2,1,0:T(2,128)} %pattern.1, s32[8,256]{1,0:T(8,128)} %index.1, f32[128,128]{1,0:T(8,128)} %bitcast.5, f32[32,8,256]{2,1,0:T(8,128)} %base_in.1, ...), custom_call_target="tpu_custom_call" | custom-call | tf_op jit(solution)/shard_map/pallas_call | solution.py:548
  77.7 1.8 %shard_map.166 = (f32[2,3072]{1,0:T(2,128)}, f32[32,8,256]{2,1,0:T(8,128)}, f32[2,3072]{1,0:T(2,128)}, f32[2]{0:T(128)}) custom-call(f32[2,3072]{1,0:T(2,128)} %get-tuple-element.8.levels, f32[32,2048]{1,0:T(8,128)} %get-tuple-element.9.dual, f32[2,3072]{1,0:T(2,128)} %get-tuple-element.10.ramp, f32[8,128]{1,0:T(8,128)} %get-tuple-element.11.price), custom_call_target="tpu_custom_call" | custom-call | tf_op jit(solution)/shard_map/pallas_call | solution.py:608

commit v4 on v3

--- a/solution.py
+++ b/solution.py
@@ -76,53 +76,6 @@
             barrier, inc=1, device_id={"ctg": lax.rem(me + d, n)}, device_id_type=pl.DeviceIdType.MESH
         )
 
-    pl.semaphore_wait(barrier, n - 1)
-
-    def frag_copy(c, target):
-        return send(
-            starts.at[:, :, pl.ds(pl.multiple_of(c * width, 128), width)],
-            start_stage.at[home_row], frag_send.at[c], frag_recv.at[home_row], target,
-        )
-
-    starts[0] = level_in[...]
-    starts[1] = cost_in[...]
-    starts[2] = ramp_in[...]
-    for c in range(chunks):
-        target = c * groups + home_group
-
-        @pl.when(target != me)
-        def _():
-            frag_copy(c, target).start()
-
-        @pl.when(target == me)
-        def _():
-            start_stage[home_row] = starts[:, :, c * width:(c + 1) * width]
-
-    def stat_copy(slot, target, sender):
-        return send(
-            stats.at[slot, sender], stats.at[slot, sender],
-            stat_send.at[slot % 2, target], stat_recv.at[slot % 2, sender], target,
-        )
-
-    def stat_start(slot):
-        @pl.loop(1, n)
-        def _(d):
-            stat_copy(slot, lax.rem(me + d, n), me).start()
-
-    def stat_wait(slot):
-        @pl.loop(1, n)
-        def _(d):
-            peer = lax.rem(me + d, n)
-            stat_copy(slot, peer, me).wait_send()
-            stat_copy(slot, peer, peer).wait_recv()
-
-    hour = lax.broadcasted_iota(jnp.int32, (8, 128), 1) - me * hour_rows
-    own_demand = jnp.zeros((8, 128), f32)
-    for r in range(hour_rows):
-        own_demand = jnp.where(hour == r, demand[r], own_demand)
-    stats[0, me] = own_demand
-    stat_start(0)
-
     row_iota = lax.broadcasted_iota(jnp.int32, (128, lines), 0)
     values = table[...].T
     part_a = values.astype(bf16)
@@ -152,6 +105,53 @@
     omega[...] = jnp.ones_like(omega)
     price[...] = jnp.zeros_like(price)
 
+    pl.semaphore_wait(barrier, n - 1)
+
+    def frag_copy(c, target):
+        return send(
+            starts.at[:, :, pl.ds(pl.multiple_of(c * width, 128), width)],
+            start_stage.at[home_row], frag_send.at[c], frag_recv.at[home_row], target,
+        )
+
+    starts[0] = level_in[...]
+    starts[1] = cost_in[...]
+    starts[2] = ramp_in[...]
+    for c in range(chunks):
+        target = c * groups + home_group
+
+        @pl.when(target != me)
+        def _():
+            frag_copy(c, target).start()
+
+        @pl.when(target == me)
+        def _():
+            start_stage[home_row] = starts[:, :, c * width:(c + 1) * width]
+
+    def stat_copy(slot, target, sender):
+        return send(
+            stats.at[slot, sender], stats.at[slot, sender],
+            stat_send.at[slot % 2, target], stat_recv.at[slot % 2, sender], target,
+        )
+
+    def stat_start(slot):
+        @pl.loop(1, n)
+        def _(d):
+            stat_copy(slot, lax.rem(me + d, n), me).start()
+
+    def stat_wait(slot):
+        @pl.loop(1, n)
+        def _(d):
+            peer = lax.rem(me + d, n)
+            stat_copy(slot, peer, me).wait_send()
+            stat_copy(slot, peer, peer).wait_recv()
+
+    hour = lax.broadcasted_iota(jnp.int32, (4, 128), 1) - me * hour_rows
+    own_demand = jnp.zeros((4, 128), f32)
+    for r in range(hour_rows):
+        own_demand = jnp.where(hour == r, demand[r], own_demand)
+    stats[0, me] = own_demand
+    stat_start(0)
+
     tile_count = unit_count // 128
     tile_row = lax.broadcasted_iota(jnp.int32, (tile_count, unit_count), 0)
     tile_lane = lax.broadcasted_iota(jnp.int32, (tile_count, unit_count), 1)
@@ -199,7 +199,26 @@
     row_here = lax.broadcasted_iota(jnp.int32, (ROWS, 128), 0) + my_group * ROWS
     diagonal = lane_here == row_here
     hour_lanes = lax.broadcasted_iota(jnp.int32, (1, 128), 1) < hours
-    stat_row = lax.broadcasted_iota(jnp.int32, (8, 128), 0)
+    stat_row = lax.broadcasted_iota(jnp.int32, (4, 128), 0)
+
+    ahead = 1 - lax.div(my_pair, pairs // 2)
+
+    def flip(place, length):
+        return ahead * (length - 1 - place) + (1 - ahead) * place
+
+    def skip(place, own, length):
+        return place + lax.div(place + length - own, length)
+
+    def far_pair(j):
+        last = lax.div(j + 1, pairs)
+        place = flip(skip(j, flip(my_pair, pairs), pairs), pairs)
+        return last * my_pair + (1 - last) * place
+
+    def near_pair(j):
+        return far_pair(pairs - 1 - j)
+
+    def far_chip(d):
+        return flip(skip(d - 1, flip(chip, chips), chips), chips)
 
     def block_rows(g):
         return pl.ds(pl.multiple_of(g * ROWS, ROWS), ROWS)
@@ -254,7 +273,7 @@
         def _(j):
             @pl.when(j < pairs)
             def _():
-                pair = lax.rem(my_pair + 1 + j, pairs)
+                pair = far_pair(j)
                 lanes = pl.ds(pl.multiple_of(pair * (2 * width), 256), 2 * width)
                 part = jnp.dot(dual_half[...], masked[:, lanes], preferred_element_type=f32).astype(bf16)
                 for side in range(2):
@@ -265,7 +284,7 @@
 
             @pl.when(j > 0)
             def _():
-                pair = lax.rem(my_pair + j, pairs)
+                pair = far_pair(j - 1)
                 for side in range(2):
                     c = pair * 2 + side
                     for h in range(groups // 2):
@@ -349,7 +368,7 @@
 
         @pl.loop(1, chips)
         def _(d):
-            ext_out(it, lax.rem(chip + d, chips) * 2 + core).start()
+            ext_out(it, far_chip(d) * 2 + core).start()
 
         ext_out(it, partner).start()
 
@@ -433,11 +452,11 @@
 
         @pl.loop(0, pairs)
         def _(j):
-            pair = lax.rem(my_pair + j, pairs)
+            pair = near_pair(j)
 
             @pl.when(j < pairs - 1)
             def _():
-                blocks_of(lax.rem(my_pair + j + 1, pairs), core, pass_on)
+                blocks_of(near_pair(j + 1), core, pass_on)
 
             blocks_of(pair, 1 - core, take)
             lanes = pl.ds(pl.multiple_of(pair * (2 * width), 256), 2 * width)
@@ -579,7 +598,7 @@
             pltpu.VMEM((chunks, hours, width), bf16),
             pltpu.VMEM((ITERS, n // 2, ROWS, width), bf16),
             pltpu.VMEM((ITERS, chunks, hours, width), bf16),
-            pltpu.VMEM((ITERS + 1, n, 8, 128), f32),
+            pltpu.VMEM((ITERS + 1, n, 4, 128), f32),
             pltpu.VMEM((8, 128), f32),
             pltpu.VMEM((8, 128), f32),
             sem((ctgs,)),

time: 79.7 us -> 78.3 us (0.982)
  Pallas kernels: 78.9 us -> 77.5 us
    pallas_call x1, Pallas kernels: 77.1 us -> 75.7 us  [body(): pl.pallas_call(functools.partial(kernel, n, hour_rows, step_size, balance...]
where the time goes in v4:
time: 78.3 us; the launch traced here: 78.1 us
  Pallas kernels  77.5 us (99%)
    pallas_call x1, Pallas kernels, body(): pl.pallas_call(functools.partial(kernel, n, hour_rows, step_size, balance...  75.7 us
    pallas_call x1, Pallas kernels, body(): pl.pallas_call(finish, out_shape=(jax.ShapeDtypeStruct((hour_rows, unit_c...  1.76 us

profile of v4, /device:TPU:0, one launch (start us, length us, event | category | flops | bytes accessed | tf_op | source)
XLA Modules:
  0.0 78.1 jit_solution(3898562559383266573)
XLA Ops:
  0.6 75.7 %shard_map.165 = (f32[2,3072]{1,0:T(2,128)}, f32[32,2048]{1,0:T(8,128)}, f32[2,3072]{1,0:T(2,128)}, f32[8,128]{1,0:T(8,128)}) custom-call(bf16[8,256,3072]{2,1,0:T(8,128)(2,1)} %tiles.1, s32[8,2,24]{2,1,0:T(2,128)} %pattern.1, s32[8,256]{1,0:T(8,128)} %index.1, f32[128,128]{1,0:T(8,128)} %bitcast.5, f32[32,8,256]{2,1,0:T(8,128)} %base_in.1, ...), custom_call_target="tpu_custom_call" | custom-call | tf_op jit(solution)/shard_map/pallas_call | solution.py:567
  76.4 1.8 %shard_map.166 = (f32[2,3072]{1,0:T(2,128)}, f32[32,8,256]{2,1,0:T(8,128)}, f32[2,3072]{1,0:T(2,128)}, f32[2]{0:T(128)}) custom-call(f32[2,3072]{1,0:T(2,128)} %get-tuple-element.8.levels, f32[32,2048]{1,0:T(8,128)} %get-tuple-element.9.dual, f32[2,3072]{1,0:T(2,128)} %get-tuple-element.10.ramp, f32[8,128]{1,0:T(8,128)} %get-tuple-element.11.price), custom_call_target="tpu_custom_call" | custom-call | tf_op jit(solution)/shard_map/pallas_call | solution.py:627
